TPU v7x, 32 devices: a whole 2x2x4 slice. The times are simulated.
32 devices in a mesh: row: 16 (over z, x, core), col: 2 (over y).
Axes of the slice: x: 2, y: 2, z: 4, core: 2. Of those that a mesh axis runs over, the one named last changes fastest.
Arguments:
- dosage: bfloat16 [128, 24576], P(('row', 'col')), may hold values from 0 to 2
- phenos: bfloat16 [16, 24576], P(None, 'col'), may hold values from -6 to 6
Outputs:
- grm: float32 [24576, 24576], P('row', 'col')
- projected: float32 [16, 24576], P(None, ('row', 'col'))
All inputs are finite; a program needn't handle non-finite values.
Results may differ from a plain program's by a relative error of at most 0.0049.
Values may be sent and summed in bfloat16 or wider, within the bound.
A program may use at most 192 MiB of HBM per device.

v0:
```python
import jax
import jax.numpy as jnp
from jax import lax
from jax.sharding import PartitionSpec as P

eps = 1e-05


def standardize(dosage):
    values = dosage.astype(jnp.float32)
    site_mean = jnp.mean(values, axis=1, keepdims=True)
    centred = values - site_mean
    site_var = jnp.mean(centred * centred, axis=1, keepdims=True)
    return (centred * lax.rsqrt(site_var + eps)).astype(jnp.bfloat16)


def per_device(dosage, phenos):
    standard = standardize(dosage)
    regrouped = lax.all_to_all(standard, "row", split_axis=1, concat_axis=0, tiled=True)
    row_raw = lax.all_gather(regrouped, "col", axis=0, tiled=True)
    snp_total = row_raw.shape[0]
    col_wide = lax.all_gather(standard, "row", axis=0, tiled=True)
    col_block = lax.all_to_all(col_wide, "col", split_axis=1, concat_axis=0, tiled=True)
    grm_tile = lax.dot_general(
        row_raw, col_block, (((0,), (0,)), ((), ())), preferred_element_type=jnp.float32
    ) * (1.0 / snp_total)
    grm_half = grm_tile.astype(jnp.bfloat16)
    partial_value = lax.dot_general(
        phenos, grm_half, (((1,), (1,)), ((), ())), preferred_element_type=jnp.float32
    )
    projected = lax.psum_scatter(partial_value, "col", scatter_dimension=1, tiled=True)
    return (grm_tile, projected)


def solution(mesh):
    placed = (P(("row", "col"), None), P(None, "col"))
    return jax.shard_map(
        per_device,
        mesh=mesh,
        in_specs=placed,
        out_specs=(P("row", "col"), P(None, ("row", "col"))),
        check_vma=False,
    )
```

profile of v0, /device:TPU:1, one launch (start us, length us, event | category | flops | bytes accessed | tf_op | source)
XLA Modules:
  0.0 186.6 jit_solution(9419165912140708585)
XLA Ops:
  7.2 0.0 copy-start
  7.2 0.0 all-gather.3.cloned.1.call-start
  7.2 1.3 convert_reduce_fusion
  8.5 1.3 fusion.7
  9.8 1.8 fusion.12
  11.6 0.0 all-gather.3.cloned.1.call-update
  11.6 1.8 fusion.8
  13.4 7.3 %all-to-all-start = ((bf16[4,16,1536]{2,0,1:T(4,128)(2,1)}), bf16[4,16,1536]{2,0,1:T(4,128)(2,1)}, u32[]{:S(2)}, u32[]{:S(2)}) async-start(bf16[4,16,1536]{2,0,1:T(4,128)(2,1)} %bitcast), calls=%async_computation | async-start | bytes 393216 | tf_op jit(solution)/shard_map/all_to_all | solution.py:19
  20.7 40.9 %all-gather.3.cloned.1.call-done = bf16[16,4,24576]{2,1,0:T(4,128)(2,1)} async-done(((bf16[1,4,24576]{2,1,0:T(4,128)(2,1)}), bf16[16,4,24576]{2,1,0:T(4,128)(2,1)}) %all-gather.3.cloned.1.call-update) | async-done | bytes 3145744 | tf_op jit(solution)/shard_map/all_gather | solution.py:22
  61.6 7.1 %all_to_all.32 = bf16[64,2,12288]{2,1,0:T(2,128)(2,1)S(1)} reshape(bf16[16,4,24576]{2,1,0:T(4,128)(2,1)} %all-gather.3.cloned.1.call-done) | data formatting | bytes 6291456 | tf_op jit(solution)/shard_map/all_to_all | solution.py:23
  68.7 3.4 %copy.8 = bf16[64,2,12288]{2,0,1:T(8,128)(2,1)} copy(bf16[64,2,12288]{2,1,0:T(2,128)(2,1)S(1)} %all_to_all.32) | data formatting | bytes 6291456 | tf_op jit(solution)/shard_map/all_to_all | solution.py:23
  72.1 0.0 all-to-all-done
  72.1 3.9 %all-to-all-start.1 = ((bf16[64,2,12288]{2,0,1:T(8,128)(2,1)}), bf16[64,2,12288]{2,0,1:T(8,128)(2,1)S(1)}, u32[]{:S(2)}, u32[]{:S(2)}) async-start(bf16[64,2,12288]{2,0,1:T(8,128)(2,1)} %copy.8), calls=%async_computation.1 | async-start | bytes 6291456 | tf_op jit(solution)/shard_map/all_to_all | solution.py:23
  76.1 0.0 reduce-scatter.2.cloned.1.call-start
  76.1 1.7 all_to_all.31
  77.8 38.5 %all_gather.6 = bf16[128,1536]{1,0:T(8,128)(2,1)} all-gather(bf16[64,1536]{1,0:T(8,128)(2,1)} %all_to_all.31), channel_id=1, replica_groups=mesh['row'=16,'col'=2] {'col'}, dimensions={0}, use_global_device_ids=true | all-gather | bytes 589824 | tf_op jit(solution)/shard_map/all_gather | solution.py:20
  116.3 0.0 all-to-all-done.1
  116.3 29.2 %convolution_multiply_fusion = f32[1536,12288]{1,0:T(8,128)} fusion(bf16[128,1536]{1,0:T(8,128)(2,1)} %all_gather.6, bf16[128,12288]{1,0:T(8,128)(2,1)S(1)} %bitcast.12), kind=kOutput, calls=%fused_computation | convolution fusion | flops 4850712576 | bytes 79036416 | tf_op jit(solution)/shard_map/dot_general | solution.py:24
  145.5 0.0 copy-done
  145.5 25.9 %fusion.2 = f32[16,1536]{1,0:T(8,128)} fusion(bf16[16,12288]{1,0:T(8,128)(2,1)S(1)} %copy-done, f32[1536,12288]{1,0:T(8,128)} %convolution_multiply_fusion), kind=kOutput, calls=%fused_computation.3 | convolution fusion | flops 622854144 | bytes 75988992 | tf_op jit(solution)/shard_map/dot_general | solution.py:28
  171.4 0.0 reduce-scatter.2.cloned.1.call-update
  171.5 8.3 %reduce-scatter.2.cloned.1.call-done = f32[16,768]{1,0:T(8,128)} async-done(((f32[16,1536]{1,0:T(8,128)}), f32[16,768]{1,0:T(8,128)}) %reduce-scatter.2.cloned.1.call-update) | async-done | bytes 49168 | tf_op jit(solution)/shard_map/reduce_scatter | solution.py:31
  (2 shorter events, 0.0 us)
Async XLA Ops:
  7.2 138.4 %copy-start = (bf16[16,12288]{1,0:T(8,128)(2,1)S(1)}, bf16[16,12288]{1,0:T(8,128)(2,1)}, u32[]{:S(2)}) copy-start(bf16[16,12288]{1,0:T(8,128)(2,1)} %param.3) | copy-start | bytes 1179652
  7.2 54.4 %all-gather.3.cloned.1.call-start = ((), (), s32[]{:S(2)}) async-start(), calls=%async_computation.4 | async-start | bytes 3342336 | tf_op jit(solution)/shard_map/all_gather | solution.py:22
  13.4 58.7 %all-to-all-start = ((bf16[4,16,1536]{2,0,1:T(4,128)(2,1)}), bf16[4,16,1536]{2,0,1:T(4,128)(2,1)}, u32[]{:S(2)}, u32[]{:S(2)}) async-start(bf16[4,16,1536]{2,0,1:T(4,128)(2,1)} %bitcast), calls=%async_computation | async-start | bytes 393216 | tf_op jit(solution)/shard_map/all_to_all | solution.py:19
  72.1 44.2 %all-to-all-start.1 = ((bf16[64,2,12288]{2,0,1:T(8,128)(2,1)}), bf16[64,2,12288]{2,0,1:T(8,128)(2,1)S(1)}, u32[]{:S(2)}, u32[]{:S(2)}) async-start(bf16[64,2,12288]{2,0,1:T(8,128)(2,1)} %copy.8), calls=%async_computation.1 | async-start | bytes 6291456 | tf_op jit(solution)/shard_map/all_to_all | solution.py:23
  76.1 103.7 %reduce-scatter.2.cloned.1.call-start = ((), (), s32[]{:S(2)}) async-start(), calls=%async_computation.3 | async-start | bytes 147456 | tf_op jit(solution)/shard_map/reduce_scatter | solution.py:31
Sparse Core Ops, SparseCore 0:
  11.8 49.8 all-gather.2
  171.6 8.1 reduce-scatter.1
where the time goes:
time: 188 us; the launch traced here: 187 us
  matrix products  55.1 us (29%)
  waiting for transfers between devices  49.2 us (26%)
  blocking collectives  38.5 us (20%)
  between operations  14.1 us (8%)
  local copies, waits for them, and re-layouts  12.2 us (6%)
  starting transfers between devices  11.3 us (6%)
  other arithmetic  6.16 us (3%)
    all_gather x1, waiting for transfers between devices, per_device(): col_wide = lax.all_gather(standard, 'row', axis=0, tiled=True)  40.9 us
    all_gather x1, blocking collectives, per_device(): row_raw = lax.all_gather(regrouped, 'col', axis=0, tiled=True)  38.5 us
    dot_general x1, matrix products, per_device(): lax.dot_general(row_raw, col_block, (((0,), (0,)), ((), ())), preferred_e...  29.2 us
    dot_general x1, matrix products, per_device(): lax.dot_general(phenos, grm_half, (((1,), (1,)), ((), ())), preferred_ele...  25.9 us
    all_to_all x2, local copies, waits for them, and re-layouts, per_device(): lax.all_to_all(col_wide, 'col', split_axis=1, concat_axis=0, tiled=True)  10.5 us
    reduce_scatter x1, waiting for transfers between devices, per_device(): lax.psum_scatter(partial_value, 'col', scatter_dimension=1, tiled=True)  8.3 us
    all_to_all x1, starting transfers between devices, per_device(): lax.all_to_all(standard, 'row', split_axis=1, concat_axis=0, tiled=True)  7.32 us
    all_to_all x1, starting transfers between devices, per_device(): lax.all_to_all(col_wide, 'col', split_axis=1, concat_axis=0, tiled=True)  3.95 us
  transfers between devices with their start and end apart: 4, of which 2 were waited for; matrix products, arithmetic and copies ran while one was open for 3% of the time, Pallas kernels for 0%

commit v1 on v0

v1 whole, which is shorter than its diff:
```python
import functools

import jax
import jax.numpy as jnp
from jax import lax
from jax.experimental import pallas as pl
from jax.experimental.pallas import tpu as pltpu
from jax.sharding import PartitionSpec as P

eps = 1e-05
MESH = pl.DeviceIdType.MESH


def place_of(row, depth, width):
    chip, core = row // 2, row % 2
    a, b = chip // width, chip % width
    turn = depth - 1 - a
    odd = turn % 2
    first = (width - 1 - b) // (width - 1)
    later = depth + turn * (width - 1) + (1 - odd) * (b - 1) + odd * (width - 1 - b)
    return first * a + (1 - first) * later, core


def row_at(place, core, depth, width):
    first = 1 - jnp.minimum(place // depth, 1)
    rest = jnp.maximum(place - depth, 0)
    turn, step = rest // (width - 1), rest % (width - 1)
    odd = turn % 2
    later = (depth - 1 - turn) * width + (1 - odd) * (1 + step) + odd * (width - 1 - step)
    return (first * place * width + (1 - first) * later) * 2 + core


def gather_kernel(
    rows, cols, dosage_ref, phenos_ref, col_ref, row_ref, weight_ref,
    mine, swapped, parts, swap_send, swap_recv, ring_send, ring_recv, sib_send, sib_recv,
    line_send, line_recv, part_send, part_recv,
):
    row, col = lax.axis_index("row"), lax.axis_index("col")
    chips = rows // 2
    depth = min(4, chips)
    width = chips // depth
    place, core = place_of(row, depth, width)
    sibling = row + 1 - 2 * core
    ahead = row_at((place + 1) % chips, core, depth, width)
    behind = row_at((place + chips - 1) % chips, core, depth, width)
    sites = dosage_ref.shape[0]
    wide = col_ref.shape[2]
    half = wide // 2
    tall = row_ref.shape[2]
    per_col = rows // cols
    home = row // per_col
    offset = pl.multiple_of((row % per_col) * tall, 128)

    barrier = pltpu.get_barrier_semaphore()
    for other in (ahead, behind, sibling):
        pl.semaphore_signal(barrier, inc=1, device_id=(other, col), device_id_type=MESH)
    for k in range(1, cols):
        pl.semaphore_signal(
            barrier, inc=1, device_id=(row, (col + k) % cols), device_id_type=MESH
        )

    values = dosage_ref[...].astype(jnp.float32)
    samples = values.shape[1]
    mean = jnp.sum(values, axis=1, keepdims=True) * (1.0 / samples)
    centred = values - mean
    var = jnp.sum(centred * centred, axis=1, keepdims=True) * (1.0 / samples)
    scale = lax.rsqrt(var + eps)
    for c in range(cols):
        piece = dosage_ref[:, c * wide:(c + 1) * wide].astype(jnp.float32)
        mine[c] = ((piece - mean) * scale).astype(jnp.bfloat16)

    pl.semaphore_wait(barrier, 3 + cols - 1)

    swaps = []
    for k in range(1, cols):
        target = (col + k) % cols
        swap = pltpu.make_async_remote_copy(
            src_ref=mine.at[target], dst_ref=swapped.at[col],
            send_sem=swap_send.at[k - 1], recv_sem=swap_recv.at[k - 1],
            device_id=(row, target), device_id_type=MESH,
        )
        swap.start()
        swaps.append(swap)
    swapped[col] = mine[col]
    for swap in swaps:
        swap.wait_recv()
    for c in range(cols):
        col_ref[row, c * sites:(c + 1) * sites, :] = swapped[c]

    def ring_copy(direction, step, part, source):
        lane = pl.ds(part * half, half)
        target = ahead if direction == 0 else behind
        where = col_ref.at[source, :, lane]
        return pltpu.make_async_remote_copy(
            src_ref=where, dst_ref=where,
            send_sem=ring_send.at[direction, step, part],
            recv_sem=ring_recv.at[direction, step, part],
            device_id=(target, col), device_id_type=MESH,
        )

    def sib_copy(index, source):
        where = col_ref.at[source]
        return pltpu.make_async_remote_copy(
            src_ref=where, dst_ref=where,
            send_sem=sib_send.at[index], recv_sem=sib_recv.at[index],
            device_id=(sibling, col), device_id_type=MESH,
        )

    def line_copy(source, k):
        return pltpu.make_async_remote_copy(
            src_ref=col_ref.at[source, :, pl.ds(offset, tall)], dst_ref=row_ref.at[source],
            send_sem=line_send.at[source, k - 1], recv_sem=line_recv.at[source],
            device_id=(row, (col + k) % cols), device_id_type=MESH,
        )

    def lines(source):
        @pl.when(home == col)
        def _():
            for k in range(1, cols):
                line_copy(source, k).start()
            row_ref[source] = col_ref[source, :, pl.ds(offset, tall)]

    steps = chips // 2
    sent = []

    def launch(copy):
        copy.start()
        sent.append(copy)

    def routes(step):
        if step < steps - 1:
            return [(0, 0), (1, 1), (0, 1), (1, 0)]
        return [(0, 0), (1, 1)]

    for direction, part in routes(0):
        launch(ring_copy(direction, 0, part, row))
    launch(sib_copy(0, row))
    lines(row)
    waiting = [(0, sibling)]
    count = 1
    for step in range(steps):
        sources = (
            row_at((place + 2 * chips - step - 1) % chips, core, depth, width),
            row_at((place + step + 1) % chips, core, depth, width),
        )
        for direction, part in routes(step):
            ring_copy(direction, step, part, sources[direction]).wait_recv()
            if step + 1 < steps and (direction, part) in routes(step + 1):
                launch(ring_copy(direction, step + 1, part, sources[direction]))
        for source in sources if step < steps - 1 else sources[:1]:
            launch(sib_copy(count, source))
            lines(source)
            waiting.append((count, source + 1 - 2 * core))
            count += 1
        due = waiting[:-2] if step < steps - 1 else waiting
        waiting = waiting[len(due):]
        for index, source in due:
            sib_copy(index, source).wait_recv()
            lines(source)

    block = col_ref.shape[1]
    product = lax.dot_general(
        phenos_ref[...], col_ref[...].reshape(rows * block, wide),
        (((1,), (1,)), ((), ())), preferred_element_type=jnp.float32,
    )
    parts[0] = product
    trades = []
    for k in range(1, cols):
        trade = pltpu.make_async_remote_copy(
            src_ref=parts.at[0], dst_ref=parts.at[k],
            send_sem=part_send.at[k - 1], recv_sem=part_recv.at[k - 1],
            device_id=(row, (col + k) % cols), device_id_type=MESH,
        )
        trade.start()
        trades.append(trade)

    @pl.when(home != col)
    def _():
        def take(source, carry):
            line_copy(source, 1).wait_recv()
            return carry
        lax.fori_loop(0, rows, take, 0)

    @pl.when(home == col)
    def _():
        def take(source, carry):
            for k in range(1, cols):
                line_copy(source, k).wait_send()
            return carry
        lax.fori_loop(0, rows, take, 0)

    total = parts[0]
    for k in range(1, cols):
        trades[k - 1].wait_recv()
        total = total + parts[k]
    weight_ref[...] = total
    for copy in swaps + sent + trades:
        copy.wait_send()


def product_kernel(cols, row_ref, col_ref, weight_ref, grm_ref, projected_ref):
    sites = row_ref.shape[0]

    @pl.when(pl.program_id(0) == 0)
    def _():
        part = projected_ref.shape[1]
        col = lax.axis_index("col")
        lane = pl.ds(pl.multiple_of(col * part, 128), part)
        projected_ref[...] = jnp.dot(
            weight_ref[...], row_ref[:, lane].astype(jnp.float32),
            precision=lax.Precision.HIGHEST, preferred_element_type=jnp.float32,
        ) * (1.0 / sites)

    tall = grm_ref.shape[0]
    lines = pl.ds(pl.multiple_of(pl.program_id(0) * tall, 128), tall)
    grm_ref[...] = lax.dot_general(
        row_ref[:, lines], col_ref[...], (((0,), (0,)), ((), ())),
        preferred_element_type=jnp.float32,
    ) * (1.0 / sites)


def per_device(rows, cols, dosage, phenos):
    sites, samples = dosage.shape
    count = phenos.shape[0]
    block, wide, tall = sites * cols, samples // cols, samples // rows
    total = rows * block
    vmem = pl.BlockSpec(memory_space=pltpu.VMEM)
    dma = pltpu.SemaphoreType.DMA
    chips = rows // 2
    others = cols - 1
    col_block, row_block, weight = pl.pallas_call(
        functools.partial(gather_kernel, rows, cols),
        out_shape=[
            jax.ShapeDtypeStruct((rows, block, wide), jnp.bfloat16),
            jax.ShapeDtypeStruct((rows, block, tall), jnp.bfloat16),
            jax.ShapeDtypeStruct((count, total), jnp.float32),
        ],
        in_specs=[vmem, vmem],
        out_specs=[vmem, vmem, vmem],
        scratch_shapes=[
            pltpu.VMEM((cols, sites, wide), jnp.bfloat16),
            pltpu.VMEM((cols, sites, wide), jnp.bfloat16),
            pltpu.VMEM((cols, count, total), jnp.float32),
            dma((others,)), dma((others,)),
            dma((2, chips // 2, 2)), dma((2, chips // 2, 2)),
            dma((chips,)), dma((chips,)),
            dma((rows, others)), dma((rows,)),
            dma((others,)), dma((others,)),
        ],
        compiler_params=pltpu.CompilerParams(
            collective_id=0, has_side_effects=True, vmem_limit_bytes=48 * 2**20
        ),
        name="gather",
    )(dosage, phenos)
    row_block = row_block.reshape(total, tall)
    col_block = col_block.reshape(total, wide)
    lines = 128
    grm, projected = pl.pallas_call(
        functools.partial(product_kernel, cols),
        grid=(tall // lines,),
        out_shape=[
            jax.ShapeDtypeStruct((tall, wide), jnp.float32),
            jax.ShapeDtypeStruct((count, tall // cols), jnp.float32),
        ],
        in_specs=[vmem, vmem, vmem],
        out_specs=[
            pl.BlockSpec((lines, wide), lambda i: (i, 0)),
            pl.BlockSpec((count, tall // cols), lambda i: (0, 0)),
        ],
        compiler_params=pltpu.CompilerParams(vmem_limit_bytes=48 * 2**20),
        name="product",
    )(row_block, col_block, weight)
    return grm, projected


def solution(mesh):
    rows, cols = mesh.shape["row"], mesh.shape["col"]
    return jax.shard_map(
        functools.partial(per_device, rows, cols),
        mesh=mesh,
        in_specs=(P(("row", "col"), None), P(None, "col")),
        out_specs=(P("row", "col"), P(None, ("row", "col"))),
        check_vma=False,
    )
```

time: 188 us -> 57.4 us (0.31)
  matrix products: 55.1 us -> 0 us
  Pallas kernels: 0 us -> 54.7 us
  waiting for transfers between devices: 49.2 us -> 0 us
  blocking collectives: 38.5 us -> 0 us
  between operations: 14.1 us -> 0.65 us
  starting transfers between devices: 11.3 us -> 0 us
  local copies, waits for them, and re-layouts: 12.2 us -> 1.92 us
  other arithmetic: 6.16 us -> 0 us
    dot_general x2 -> x0, matrix products: 55.1 us -> none  [the longest x1 29.2 us: per_device(): lax.dot_general(row_raw, col_block, (((0,), (0,)), ((), ())), preferred_e...]
    pallas_call x0 -> x2, Pallas kernels: none -> 54.7 us  [the longest x1 29.7 us: per_device(): pl.pallas_call(functools.partial(gather_kernel, rows, cols), out_shape=[j...]
    all_gather x1 -> x0, waiting for transfers between devices: 40.9 us -> none  [per_device(): col_wide = lax.all_gather(standard, 'row', axis=0, tiled=True)]
    all_gather x1 -> x0, blocking collectives: 38.5 us -> none  [per_device(): row_raw = lax.all_gather(regrouped, 'col', axis=0, tiled=True)]
    all_to_all x3 -> x0, local copies, waits for them, and re-layouts: 12.1 us -> none  [the longest x2 10.5 us: per_device(): lax.all_to_all(col_wide, 'col', split_axis=1, concat_axis=0, tiled=True)]
    all_to_all x2 -> x0, starting transfers between devices: 11.3 us -> none  [the longest x1 7.32 us: per_device(): lax.all_to_all(standard, 'row', split_axis=1, concat_axis=0, tiled=True)]
    reduce_scatter x1 -> x0, waiting for transfers between devices: 8.3 us -> none  [per_device(): lax.psum_scatter(partial_value, 'col', scatter_dimension=1, tiled=True)]
    reduce_sum x2 -> x0, other arithmetic: 2.6 us -> none  [the longest x1 1.31 us: standardize(): site_var = jnp.mean(centred * centred, axis=1, keepdims=True)]
  transfers between devices with their start and end apart: 4 -> 0, of which waited for: 2 -> 0; matrix products, arithmetic and copies ran while one was open for 3% -> 0% of each run, Pallas kernels for 0% -> 0%
where the time goes in v1:
time: 57.4 us; the launch traced here: 57.3 us
  Pallas kernels  54.7 us (95%)
  local copies, waits for them, and re-layouts  1.92 us (3%)
  between operations  0.65 us (1%)
    pallas_call x1, Pallas kernels, per_device(): pl.pallas_call(functools.partial(gather_kernel, rows, cols), out_shape=[j...  29.7 us
    pallas_call x1, Pallas kernels, per_device(): pl.pallas_call(functools.partial(product_kernel, cols), grid=(tall // lin...  25 us
    unnamed x4, local copies, waits for them, and re-layouts  1.92 us

profile of v1, /device:TPU:1, one launch (start us, length us, event | category | flops | bytes accessed | tf_op | source)
XLA Modules:
  0.0 57.3 jit_solution(9432150221348489706)
XLA Ops:
  0.6 0.0 copy-start
  0.6 1.0 %copy-done = bf16[16,12288]{1,0:T(8,128)(2,1)S(1)} copy-done((bf16[16,12288]{1,0:T(8,128)(2,1)S(1)}, bf16[16,12288]{1,0:T(8,128)(2,1)}, u32[]{:S(2)}) %copy-start) | copy-done | bytes 393240
  1.6 0.0 copy-start.1
  1.6 0.9 %copy-done.1 = bf16[4,24576]{1,0:T(4,128)(2,1)S(1)} copy-done((bf16[4,24576]{1,0:T(4,128)(2,1)S(1)}, bf16[4,24576]{1,0:T(4,128)(2,1)}, u32[]{:S(2)}) %copy-start.1) | copy-done | bytes 196632
  2.6 29.7 %gather.1 = (bf16[16,8,12288]{2,1,0:T(8,128)(2,1)S(1)}, bf16[16,8,1536]{2,1,0:T(8,128)(2,1)S(1)}, f32[16,128]{1,0:T(8,128)S(1)}) custom-call(bf16[4,24576]{1,0:T(4,128)(2,1)S(1)} %copy-done.1, bf16[16,12288]{1,0:T(8,128)(2,1)S(1)} %copy-done), custom_call_target="tpu_custom_call" | custom-call | tf_op jit(solution)/shard_map/gather/pallas_call | solution.py:231
  32.2 25.0 %product.1 = (f32[1536,12288]{1,0:T(8,128)}, f32[16,768]{1,0:T(8,128)}) custom-call(bf16[128,1536]{1,0:T(8,128)(2,1)S(1)} %bitcast.3, bf16[128,12288]{1,0:T(8,128)(2,1)S(1)} %bitcast.2, f32[16,128]{1,0:T(8,128)S(1)} %get-tuple-element.7.weight_ref), custom_call_target="tpu_custom_call" | custom-call | tf_op jit(solution)/shard_map/product/pallas_call | solution.py:258
Async XLA Ops:
  0.6 1.0 %copy-start = (bf16[16,12288]{1,0:T(8,128)(2,1)S(1)}, bf16[16,12288]{1,0:T(8,128)(2,1)}, u32[]{:S(2)}) copy-start(bf16[16,12288]{1,0:T(8,128)(2,1)} %phenos_ref.1) | copy-start | bytes 1179652
  1.6 0.9 %copy-start.1 = (bf16[4,24576]{1,0:T(4,128)(2,1)S(1)}, bf16[4,24576]{1,0:T(4,128)(2,1)}, u32[]{:S(2)}) copy-start(bf16[4,24576]{1,0:T(4,128)(2,1)} %dosage_ref.1) | copy-start | bytes 589828

commit v2 on v1

--- a/solution.py
+++ b/solution.py
@@ -32,7 +32,7 @@
 
 def gather_kernel(
     rows, cols, dosage_ref, phenos_ref, col_ref, row_ref, weight_ref,
-    mine, swapped, parts, swap_send, swap_recv, ring_send, ring_recv, sib_send, sib_recv,
+    mine, pieces, parts, swap_send, swap_recv, ring_send, ring_recv, sib_send, sib_recv,
     line_send, line_recv, part_send, part_recv,
 ):
     row, col = lax.axis_index("row"), lax.axis_index("col")
@@ -45,7 +45,6 @@
     behind = row_at((place + chips - 1) % chips, core, depth, width)
     sites = dosage_ref.shape[0]
     wide = col_ref.shape[2]
-    half = wide // 2
     tall = row_ref.shape[2]
     per_col = rows // cols
     home = row // per_col
@@ -65,38 +64,46 @@
     centred = values - mean
     var = jnp.sum(centred * centred, axis=1, keepdims=True) * (1.0 / samples)
     scale = lax.rsqrt(var + eps)
-    for c in range(cols):
-        piece = dosage_ref[:, c * wide:(c + 1) * wide].astype(jnp.float32)
-        mine[c] = ((piece - mean) * scale).astype(jnp.bfloat16)
-
-    pl.semaphore_wait(barrier, 3 + cols - 1)
+
+    def standard(c):
+        lane = pl.ds(pl.multiple_of(c * wide, 128), wide)
+        piece = dosage_ref[:, lane].astype(jnp.float32)
+        return ((piece - mean) * scale).astype(jnp.bfloat16)
+
+    steps = chips // 2
+    sent = []
+
+    def launch(copy):
+        copy.start()
+        sent.append(copy)
 
     swaps = []
     for k in range(1, cols):
         target = (col + k) % cols
+        mine[k - 1] = standard(target)
+        if k == 1:
+            pl.semaphore_wait(barrier, 3 + cols - 1)
         swap = pltpu.make_async_remote_copy(
-            src_ref=mine.at[target], dst_ref=swapped.at[col],
+            src_ref=mine.at[k - 1], dst_ref=pieces.at[row, col],
             send_sem=swap_send.at[k - 1], recv_sem=swap_recv.at[k - 1],
             device_id=(row, target), device_id_type=MESH,
         )
-        swap.start()
+        launch(swap)
         swaps.append(swap)
-    swapped[col] = mine[col]
-    for swap in swaps:
-        swap.wait_recv()
-    for c in range(cols):
-        col_ref[row, c * sites:(c + 1) * sites, :] = swapped[c]
-
-    def ring_copy(direction, step, part, source):
-        lane = pl.ds(part * half, half)
+
+    def ring_copy(direction, step, k, source):
         target = ahead if direction == 0 else behind
-        where = col_ref.at[source, :, lane]
+        where = pieces.at[source, (col + cols - k) % cols]
         return pltpu.make_async_remote_copy(
             src_ref=where, dst_ref=where,
-            send_sem=ring_send.at[direction, step, part],
-            recv_sem=ring_recv.at[direction, step, part],
+            send_sem=ring_send.at[direction, step, k],
+            recv_sem=ring_recv.at[direction, step, k],
             device_id=(target, col), device_id_type=MESH,
         )
+
+    def assemble(source):
+        for c in range(cols):
+            col_ref[source, c * sites:(c + 1) * sites, :] = pieces[source, c]
 
     def sib_copy(index, source):
         where = col_ref.at[source]
@@ -120,20 +127,17 @@
                 line_copy(source, k).start()
             row_ref[source] = col_ref[source, :, pl.ds(offset, tall)]
 
-    steps = chips // 2
-    sent = []
-
-    def launch(copy):
-        copy.start()
-        sent.append(copy)
-
     def routes(step):
         if step < steps - 1:
-            return [(0, 0), (1, 1), (0, 1), (1, 0)]
-        return [(0, 0), (1, 1)]
-
-    for direction, part in routes(0):
-        launch(ring_copy(direction, 0, part, row))
+            return [(d, k) for k in range(cols) for d in (0, 1)]
+        return [(2 * k // cols, k) for k in range(cols)]
+
+    pieces[row, col] = standard(col)
+    for direction, k in routes(0):
+        if k > 0 and direction == routes(0)[2 * k][0]:
+            swaps[k - 1].wait_recv()
+        launch(ring_copy(direction, 0, k, row))
+    assemble(row)
     launch(sib_copy(0, row))
     lines(row)
     waiting = [(0, sibling)]
@@ -143,11 +147,12 @@
             row_at((place + 2 * chips - step - 1) % chips, core, depth, width),
             row_at((place + step + 1) % chips, core, depth, width),
         )
-        for direction, part in routes(step):
-            ring_copy(direction, step, part, sources[direction]).wait_recv()
-            if step + 1 < steps and (direction, part) in routes(step + 1):
-                launch(ring_copy(direction, step + 1, part, sources[direction]))
+        for direction, k in routes(step):
+            ring_copy(direction, step, k, sources[direction]).wait_recv()
+            if step + 1 < steps and (direction, k) in routes(step + 1):
+                launch(ring_copy(direction, step + 1, k, sources[direction]))
         for source in sources if step < steps - 1 else sources[:1]:
+            assemble(source)
             launch(sib_copy(count, source))
             lines(source)
             waiting.append((count, source + 1 - 2 * core))
@@ -194,14 +199,14 @@
         trades[k - 1].wait_recv()
         total = total + parts[k]
     weight_ref[...] = total
-    for copy in swaps + sent + trades:
+    for copy in sent + trades:
         copy.wait_send()
 
 
-def product_kernel(cols, row_ref, col_ref, weight_ref, grm_ref, projected_ref):
+def product_kernel(row_ref, col_ref, weight_ref, grm_ref, projected_ref):
     sites = row_ref.shape[0]
 
-    @pl.when(pl.program_id(0) == 0)
+    @pl.when(pl.program_id(0) == 2)
     def _():
         part = projected_ref.shape[1]
         col = lax.axis_index("col")
@@ -238,11 +243,11 @@
         in_specs=[vmem, vmem],
         out_specs=[vmem, vmem, vmem],
         scratch_shapes=[
-            pltpu.VMEM((cols, sites, wide), jnp.bfloat16),
-            pltpu.VMEM((cols, sites, wide), jnp.bfloat16),
+            pltpu.VMEM((others, sites, wide), jnp.bfloat16),
+            pltpu.VMEM((rows, cols, sites, wide), jnp.bfloat16),
             pltpu.VMEM((cols, count, total), jnp.float32),
             dma((others,)), dma((others,)),
-            dma((2, chips // 2, 2)), dma((2, chips // 2, 2)),
+            dma((2, chips // 2, cols)), dma((2, chips // 2, cols)),
             dma((chips,)), dma((chips,)),
             dma((rows, others)), dma((rows,)),
             dma((others,)), dma((others,)),
@@ -256,7 +261,7 @@
     col_block = col_block.reshape(total, wide)
     lines = 128
     grm, projected = pl.pallas_call(
-        functools.partial(product_kernel, cols),
+        product_kernel,
         grid=(tall // lines,),
         out_shape=[
             jax.ShapeDtypeStruct((tall, wide), jnp.float32),

time: 57.4 us -> 57.2 us (level)
  no operation moved by 1% of the time
where the time goes in v2:
time: 57.2 us; the launch traced here: 57 us
  Pallas kernels  54.5 us (95%)
  local copies, waits for them, and re-layouts  1.92 us (3%)
  between operations  0.65 us (1%)
    pallas_call x1, Pallas kernels, per_device(): pl.pallas_call(functools.partial(gather_kernel, rows, cols), out_shape=[j...  29.7 us
    pallas_call x1, Pallas kernels, per_device(): pl.pallas_call(product_kernel, grid=(tall // lines,), out_shape=[jax.Shap...  24.8 us
    unnamed x4, local copies, waits for them, and re-layouts  1.92 us

profile of v2, /device:TPU:1, one launch (start us, length us, event | category | flops | bytes accessed | tf_op | source)
XLA Modules:
  0.0 57.0 jit_solution(15538703903047184596)
XLA Ops:
  0.6 0.0 copy-start
  0.6 1.0 %copy-done = bf16[16,12288]{1,0:T(8,128)(2,1)S(1)} copy-done((bf16[16,12288]{1,0:T(8,128)(2,1)S(1)}, bf16[16,12288]{1,0:T(8,128)(2,1)}, u32[]{:S(2)}) %copy-start) | copy-done | bytes 393240
  1.6 0.0 copy-start.1
  1.6 0.9 %copy-done.1 = bf16[4,24576]{1,0:T(4,128)(2,1)S(1)} copy-done((bf16[4,24576]{1,0:T(4,128)(2,1)S(1)}, bf16[4,24576]{1,0:T(4,128)(2,1)}, u32[]{:S(2)}) %copy-start.1) | copy-done | bytes 196632
  2.6 29.7 %gather.1 = (bf16[16,8,12288]{2,1,0:T(8,128)(2,1)S(1)}, bf16[16,8,1536]{2,1,0:T(8,128)(2,1)S(1)}, f32[16,128]{1,0:T(8,128)S(1)}) custom-call(bf16[4,24576]{1,0:T(4,128)(2,1)S(1)} %copy-done.1, bf16[16,12288]{1,0:T(8,128)(2,1)S(1)} %copy-done), custom_call_target="tpu_custom_call" | custom-call | tf_op jit(solution)/shard_map/gather/pallas_call | solution.py:236
  32.2 24.8 %product.1 = (f32[1536,12288]{1,0:T(8,128)}, f32[16,768]{1,0:T(8,128)}) custom-call(bf16[128,1536]{1,0:T(8,128)(2,1)S(1)} %bitcast.3, bf16[128,12288]{1,0:T(8,128)(2,1)S(1)} %bitcast.2, f32[16,128]{1,0:T(8,128)S(1)} %get-tuple-element.7.weight_ref), custom_call_target="tpu_custom_call" | custom-call | tf_op jit(solution)/shard_map/product/pallas_call | solution.py:263
Async XLA Ops:
  0.6 1.0 %copy-start = (bf16[16,12288]{1,0:T(8,128)(2,1)S(1)}, bf16[16,12288]{1,0:T(8,128)(2,1)}, u32[]{:S(2)}) copy-start(bf16[16,12288]{1,0:T(8,128)(2,1)} %phenos_ref.1) | copy-start | bytes 1179652
  1.6 0.9 %copy-start.1 = (bf16[4,24576]{1,0:T(4,128)(2,1)S(1)}, bf16[4,24576]{1,0:T(4,128)(2,1)}, u32[]{:S(2)}) copy-start(bf16[4,24576]{1,0:T(4,128)(2,1)} %dosage_ref.1) | copy-start | bytes 589828
